TPU v7x, 128 devices: a whole 4x4x4 slice. The times are simulated.
128 devices in a mesh: row: 16 (over y, x), col: 8 (over z, core).
Axes of the slice: x: 4, y: 4, z: 4, core: 2. Of those that a mesh axis runs over, the one named last changes fastest.
Arguments:
- tokens: bfloat16 [1024, 8192], P('col', 'row'), may hold values from -6 to 6
- cotangent: bfloat16 [1024, 8192], P('col', 'row'), may hold values from -1.5 to 1.5
- gate_weight: bfloat16 [8192, 14336], P('row', 'col'), may hold values from -0.0625 to 0.0625
- up_weight: bfloat16 [8192, 14336], P('row', 'col'), may hold values from -0.0625 to 0.0625
- down_weight: bfloat16 [14336, 8192], P('col', 'row'), may hold values from -0.046875 to 0.046875
Outputs:
- layer_output: bfloat16 [1024, 8192], P('col', 'row')
- input_grad: bfloat16 [1024, 8192], P('col', 'row')
- gate_weight_grad: bfloat16 [8192, 14336], P('row', 'col')
- up_weight_grad: bfloat16 [8192, 14336], P('row', 'col')
- down_weight_grad: bfloat16 [14336, 8192], P('col', 'row')
All inputs are finite; a program needn't handle non-finite values.
Results may differ from a plain program's by a relative error of at most 0.0049.
Values may be sent and summed in bfloat16 or wider, within the bound.
No kernel may reach another device: no remote copies, remote signals or barrier semaphores. Data moves between devices by JAX's collectives and lax.ppermute only.
A program may use at most 192 MiB of HBM per device.

v0:
```python
import jax
import jax.numpy as jnp
from jax import lax
from jax.sharding import PartitionSpec as P


def contract_last(left, right):
    return lax.dot_general(
        left, right, (((1,), (1,)), ((), ())), preferred_element_type=jnp.float32
    )


def contract_first(left, right):
    return lax.dot_general(
        left, right, (((0,), (0,)), ((), ())), preferred_element_type=jnp.float32
    )


def local(tokens, cotangent, gate_weight, up_weight, down_weight):
    token_panel = lax.all_gather(tokens, "col", axis=0, tiled=True)
    row_share = token_panel.shape[0] // lax.axis_size("row")
    hidden_width = gate_weight.shape[1]
    partial_sums = jnp.concatenate(
        [
            jnp.dot(token_panel, gate_weight, preferred_element_type=jnp.float32),
            jnp.dot(token_panel, up_weight, preferred_element_type=jnp.float32),
        ],
        axis=1,
    )
    joined = lax.psum(partial_sums, "row")
    gate_all = joined[:, :hidden_width]
    up_all = joined[:, hidden_width:]
    sigmoid_all = jax.nn.sigmoid(gate_all)
    silu_all = gate_all * sigmoid_all
    hidden_panel = (silu_all * up_all).astype(jnp.bfloat16)
    first_own = lax.axis_index("row") * row_share
    own_gate = lax.dynamic_slice_in_dim(gate_all, first_own, row_share, 0)
    own_up = lax.dynamic_slice_in_dim(up_all, first_own, row_share, 0)
    sigmoid_gate = lax.dynamic_slice_in_dim(sigmoid_all, first_own, row_share, 0)
    silu_gate = lax.dynamic_slice_in_dim(silu_all, first_own, row_share, 0)
    rows_in = hidden_panel
    layer_output = lax.psum_scatter(
        jnp.dot(rows_in, down_weight, preferred_element_type=jnp.float32),
        "col",
        scatter_dimension=0,
        tiled=True,
    ).astype(jnp.bfloat16)
    grad_panel = lax.all_gather(cotangent, "col", axis=0, tiled=True)
    rows_in = grad_panel
    hidden_grad = lax.psum_scatter(
        contract_last(rows_in, down_weight), "row", scatter_dimension=0, tiled=True
    )
    down_weight_grad = contract_first(hidden_panel, grad_panel).astype(jnp.bfloat16)
    silu_slope = sigmoid_gate * (1.0 + own_gate * (1.0 - sigmoid_gate))
    gate_grad = (hidden_grad * own_up * silu_slope).astype(jnp.bfloat16)
    up_grad = (hidden_grad * silu_gate).astype(jnp.bfloat16)
    gate_grad_panel, up_grad_panel = (
        lax.all_gather(gate_grad, "row", axis=0, tiled=True),
        lax.all_gather(up_grad, "row", axis=0, tiled=True),
    )
    input_grad = lax.psum_scatter(
        contract_last(gate_grad_panel, gate_weight) + contract_last(up_grad_panel, up_weight),
        "col",
        scatter_dimension=0,
        tiled=True,
    ).astype(jnp.bfloat16)
    gate_weight_grad = contract_first(token_panel, gate_grad_panel).astype(jnp.bfloat16)
    up_weight_grad = contract_first(token_panel, up_grad_panel).astype(jnp.bfloat16)
    return (layer_output, input_grad, gate_weight_grad, up_weight_grad, down_weight_grad)


def solution(mesh):
    in_specs = (P("col", "row"), P("col", "row"), P("row", "col"), P("row", "col"), P("col", "row"))
    out_specs = (
        P("col", "row"),
        P("col", "row"),
        P("row", "col"),
        P("row", "col"),
        P("col", "row"),
    )
    return jax.shard_map(local, mesh=mesh, in_specs=in_specs, out_specs=out_specs, check_vma=False)
```

profile of v0, /device:TPU:0, one launch (start us, length us, event | category | flops | bytes accessed | tf_op | source)
XLA Modules:
  0.0 531.8 jit_solution(439490304801279585)
XLA Ops:
  7.2 0.7 all-gather.5.cloned.1.call-update
  8.0 0.7 all-gather.7.cloned.1.call-update
  8.7 0.0 all-reduce.2.cloned.1.call-start
  8.7 27.0 %all-gather.5.cloned.1.call-done = bf16[1024,512]{1,0:T(8,128)(2,1)} async-done(((bf16[128,512]{1,0:T(8,128)(2,1)}), bf16[1024,512]{1,0:T(8,128)(2,1)}) %all-gather.5.cloned.1.call-update) | async-done | bytes 1048592 | tf_op jit(solution)/shard_map/all_gather | solution.py:20
  35.7 4.0 fusion.2
  39.7 2.1 fusion.3
  41.8 5.8 %pad_maximum_fusion = f32[1024,3584]{1,0:T(8,128)} fusion(f32[1024,1792]{1,0:T(8,128)S(1)} %fusion.3, f32[1024,1792]{1,0:T(8,128)S(1)} %fusion.2), kind=kLoop, calls=%fused_computation | loop fusion | flops 3670016 | bytes 29360128 | tf_op jit(solution)/shard_map/concatenate | solution.py:23
  47.7 0.0 reduce-scatter.6.cloned.1.call-start
  47.7 13.1 %all-gather.7.cloned.1.call-done = bf16[1024,512]{1,0:T(8,128)(2,1)} async-done(((bf16[128,512]{1,0:T(8,128)(2,1)}), bf16[1024,512]{1,0:T(8,128)(2,1)}) %all-gather.7.cloned.1.call-update) | async-done | bytes 1048592 | tf_op jit(solution)/shard_map/all_gather | solution.py:48
  60.8 6.3 %fusion.5 = f32[1024,1792]{1,0:T(8,128)} fusion(bf16[1024,512]{1,0:T(8,128)(2,1)} %all-gather.7.cloned.1.call-done, bf16[1792,512]{1,0:T(8,128)(2,1)S(1)} %copy-done), kind=kOutput, calls=%fused_computation.15 | convolution fusion | flops 1879048192 | bytes 10223616 | tf_op jit(solution)/shard_map/dot_general | solution.py:8
  67.1 0.0 all-gather.9.cloned.1.call-start
  67.2 195.9 %all-reduce.2.cloned.1.call-done = f32[1024,3584]{1,0:T(8,128)} async-done(((f32[1024,3584]{1,0:T(8,128)}), f32[1024,3584]{1,0:T(8,128)}) %all-reduce.2.cloned.1.call-update) | async-done | bytes 14680080 | tf_op jit(solution)/shard_map/psum | solution.py:30
  263.1 15.5 %slice_multiply_fusion = (f32[1024,1792]{1,0:T(8,128)}, f32[1024,1792]{1,0:T(8,128)}, bf16[1024,1792]{1,0:T(8,128)(2,1)}, f32[1024,1792]{1,0:T(8,128)}, f32[1024,1792]{1,0:T(8,128)}) fusion(f32[1024,3584]{1,0:T(8,128)} %all-reduce.2.cloned.1.call-done), kind=kLoop, calls=%fused_computation.11 | loop fusion | flops 11010048 | bytes 47710208 | tf_op jit(solution)/shard_map/mul | solution.py:34
  278.5 71.4 %reduce-scatter.6.cloned.1.call-done = f32[64,1792]{1,0:T(8,128)} async-done(((f32[1024,1792]{1,0:T(8,128)}), f32[64,1792]{1,0:T(8,128)}) %reduce-scatter.6.cloned.1.call-update) | async-done | bytes 458768 | tf_op jit(solution)/shard_map/reduce_scatter | solution.py:50
  349.9 2.5 multiply_convert_fusion.1
  352.4 0.0 all-gather.11.cloned.1.call-start
  352.4 0.5 all-gather.11.cloned.1.call-update
  353.0 5.5 %fusion.4 = f32[1024,512]{1,0:T(8,128)} fusion(bf16[1024,1792]{1,0:T(8,128)(2,1)} %get-tuple-element.12, bf16[1792,512]{1,0:T(8,128)(2,1)S(1)} %copy-done), kind=kOutput, calls=%fused_computation.14 | convolution fusion | flops 1879048192 | bytes 7602176 | tf_op jit(solution)/shard_map/dot_general | solution.py:43
  358.5 0.2 reduce-scatter.8.cloned.1.call-start
  358.7 42.6 %all-gather.9.cloned.1.call-done = bf16[1024,1792]{1,0:T(8,128)(2,1)} async-done(((bf16[64,1792]{1,0:T(8,128)(2,1)}), bf16[1024,1792]{1,0:T(8,128)(2,1)}) %all-gather.9.cloned.1.call-update) | async-done | bytes 3670032 | tf_op jit(solution)/shard_map/all_gather | solution.py:58
  401.3 6.0 %fusion.6 = f32[1024,512]{1,0:T(8,128)} fusion(bf16[1024,1792]{1,0:T(8,128)(2,1)} %all-gather.9.cloned.1.call-done, bf16[512,1792]{1,0:T(8,128)(2,1)} %param.7), kind=kOutput, calls=%fused_computation.16 | convolution fusion | flops 1879048192 | bytes 7602176 | tf_op jit(solution)/shard_map/dot_general | solution.py:8
  407.4 45.1 %all-gather.11.cloned.1.call-done = bf16[1024,1792]{1,0:T(8,128)(2,1)} async-done(((bf16[64,1792]{1,0:T(8,128)(2,1)}), bf16[1024,1792]{1,0:T(8,128)(2,1)}) %all-gather.11.cloned.1.call-update) | async-done | bytes 3670032 | tf_op jit(solution)/shard_map/all_gather | solution.py:59
  452.5 6.6 %convolution_add_fusion = f32[1024,512]{1,0:T(8,128)} fusion(f32[1024,512]{1,0:T(8,128)} %fusion.6, bf16[1024,1792]{1,0:T(8,128)(2,1)} %all-gather.11.cloned.1.call-done, bf16[512,1792]{1,0:T(8,128)(2,1)} %param.8), kind=kOutput, calls=%fused_computation.8 | convolution fusion | flops 1879572480 | bytes 9699328 | tf_op jit(solution)/shard_map/dot_general | solution.py:8
  459.2 5.7 %convolution_convert_fusion = bf16[1792,512]{1,0:T(8,128)(2,1)} fusion(bf16[1024,1792]{1,0:T(8,128)(2,1)} %get-tuple-element.12, bf16[1024,512]{1,0:T(8,128)(2,1)} %all-gather.7.cloned.1.call-done), kind=kOutput, calls=%fused_computation.3 | convolution fusion | flops 1879965696 | bytes 6553600 | tf_op jit(solution)/shard_map/dot_general | solution.py:14
  464.8 23.3 %reduce-scatter.4.cloned.1.call-done = f32[128,512]{1,0:T(8,128)} async-done(((f32[1024,512]{1,0:T(8,128)}), f32[128,512]{1,0:T(8,128)}) %reduce-scatter.4.cloned.1.call-update) | async-done | bytes 262160 | tf_op jit(solution)/shard_map/reduce_scatter | solution.py:42
  488.1 1.6 convert_element_type.31
  489.7 5.4 %fusion = bf16[512,1792]{0,1:T(8,128)(2,1)} fusion(bf16[1024,1792]{1,0:T(8,128)(2,1)} %all-gather.9.cloned.1.call-done, bf16[1024,512]{1,0:T(8,128)(2,1)S(1)} %copy-done.2), kind=kOutput, calls=%fused_computation.6 | convolution fusion | flops 1879965696 | bytes 6553600 | tf_op jit(solution)/shard_map/dot_general | solution.py:14
  495.1 3.8 copy.10
  498.9 5.4 %fusion.1 = bf16[512,1792]{0,1:T(8,128)(2,1)} fusion(bf16[1024,1792]{1,0:T(8,128)(2,1)} %all-gather.11.cloned.1.call-done, bf16[1024,512]{1,0:T(8,128)(2,1)S(1)} %copy-done.2), kind=kOutput, calls=%fused_computation.7 | convolution fusion | flops 1879965696 | bytes 6553600 | tf_op jit(solution)/shard_map/dot_general | solution.py:14
  504.3 3.8 copy.11
  508.1 15.2 %reduce-scatter.8.cloned.1.call-done = f32[128,512]{1,0:T(8,128)} async-done(((f32[1024,512]{1,0:T(8,128)}), f32[128,512]{1,0:T(8,128)}) %reduce-scatter.8.cloned.1.call-update) | async-done | bytes 262160 | tf_op jit(solution)/shard_map/reduce_scatter | solution.py:61
  523.3 1.6 convert_element_type.34
  (14 shorter events, 0.2 us)
Async XLA Ops:
  7.2 53.6 %copy-start = (bf16[1792,512]{1,0:T(8,128)(2,1)S(1)}, bf16[1792,512]{1,0:T(8,128)(2,1)}, u32[]{:S(2)}) copy-start(bf16[1792,512]{1,0:T(8,128)(2,1)} %param.9) | copy-start | bytes 5505028
  7.2 28.5 %all-gather.5.cloned.1.call-start = ((), (), s32[]{:S(2)}) async-start(), calls=%async_computation.3 | async-start | bytes 1179648 | tf_op jit(solution)/shard_map/all_gather | solution.py:20
  7.9 52.9 %all-gather.7.cloned.1.call-start = ((), (), s32[]{:S(2)}) async-start(), calls=%async_computation.6 | async-start | bytes 1179648 | tf_op jit(solution)/shard_map/all_gather | solution.py:48
  8.7 254.4 %all-reduce.2.cloned.1.call-start = ((), (), s32[]{:S(2)}) async-start(), calls=%async_computation.4 | async-start | bytes 29360128 | tf_op jit(solution)/shard_map/psum | solution.py:30
  35.7 4.0 copy-start.1
  35.7 4.0 copy-start.2
  47.7 302.2 %reduce-scatter.6.cloned.1.call-start = ((), (), s32[]{:S(2)}) async-start(), calls=%async_computation.7 | async-start | bytes 7798784 | tf_op jit(solution)/shard_map/reduce_scatter | solution.py:50
  67.1 334.2 %all-gather.9.cloned.1.call-start = ((), (), s32[]{:S(2)}) async-start(), calls=%async_computation.8 | async-start | bytes 3899392 | tf_op jit(solution)/shard_map/all_gather | solution.py:58
  352.4 100.1 %all-gather.11.cloned.1.call-start = ((), (), s32[]{:S(2)}) async-start(), calls=%async_computation.9 | async-start | bytes 3899392 | tf_op jit(solution)/shard_map/all_gather | solution.py:59
  353.0 135.2 %reduce-scatter.4.cloned.1.call-start = ((), (), s32[]{:S(2)}) async-start(), calls=%async_computation.5 | async-start | bytes 2359296 | tf_op jit(solution)/shard_map/reduce_scatter | solution.py:42
  358.5 164.8 %reduce-scatter.8.cloned.1.call-start = ((), (), s32[]{:S(2)}) async-start(), calls=%async_computation.10 | async-start | bytes 2359296 | tf_op jit(solution)/shard_map/reduce_scatter | solution.py:61
Sparse Core Ops, SparseCore 0:
  9.7 25.9 all-gather.4
  37.4 23.3 all-gather.6
  64.4 198.5 all-reduce.1
  266.4 83.4 reduce-scatter.5
  352.5 48.7 all-gather.8
  403.9 48.5 all-gather.10
  454.9 33.1 reduce-scatter.3
  490.5 32.7 reduce-scatter.7
where the time goes:
time: 532 us
  waiting for transfers between devices  436 us (82%)
  matrix products  47 us (9%)
  other arithmetic  27 us (5%)
  between operations  14.2 us (3%)
  local copies, waits for them, and re-layouts  7.63 us (1%)
    psum x1, waiting for transfers between devices, local(): joined = lax.psum(partial_sums, 'row')  196 us
    reduce_scatter x1, waiting for transfers between devices, local(): lax.psum_scatter(contract_last(rows_in, down_weight), 'row', scatter_dime...  71.4 us
    all_gather x1, waiting for transfers between devices, local(): lax.all_gather(up_grad, 'row', axis=0, tiled=True)  45.1 us
    all_gather x1, waiting for transfers between devices, local(): lax.all_gather(gate_grad, 'row', axis=0, tiled=True)  42.6 us
    all_gather x1, waiting for transfers between devices, local(): token_panel = lax.all_gather(tokens, 'col', axis=0, tiled=True)  27 us
    reduce_scatter x1, waiting for transfers between devices, local(): lax.psum_scatter(jnp.dot(rows_in, down_weight, preferred_element_type=jnp...  23.3 us
    dot_general x3, matrix products, contract_last(): lax.dot_general(left, right, (((1,), (1,)), ((), ())), preferred_element_...  19 us
    dot_general x3, matrix products, contract_first(): lax.dot_general(left, right, (((0,), (0,)), ((), ())), preferred_element_...  16.4 us
  transfers between devices with their start and end apart: 8, of which 8 were waited for; matrix products, arithmetic and copies ran while one was open for 15% of the time, Pallas kernels for 0%

commit v1 on v0

--- a/solution.py
+++ b/solution.py
@@ -27,7 +27,9 @@
         ],
         axis=1,
     )
-    joined = lax.psum(partial_sums, "row")
+    joined = partial_sums
+    for hop in (1, 2, 4, 8):
+        joined = joined + lax.ppermute(joined, "row", [(dev, dev ^ hop) for dev in range(16)])
     gate_all = joined[:, :hidden_width]
     up_all = joined[:, hidden_width:]
     sigmoid_all = jax.nn.sigmoid(gate_all)

time: 532 us -> 1590 us (2.99)
  waiting for transfers between devices: 436 us -> 1440 us
  other arithmetic: 27 us -> 73.5 us
    ppermute x0 -> x4, waiting for transfers between devices: none -> 1280 us  [local(): lax.ppermute(joined, 'row', [(dev, dev ^ hop) for dev in range(16)])]
    psum x1 -> x0, waiting for transfers between devices: 196 us -> none  [local(): joined = lax.psum(partial_sums, 'row')]
    reduce_scatter x1, waiting for transfers between devices: 71.4 us -> 0.01 us  [local(): lax.psum_scatter(contract_last(rows_in, down_weight), 'row', scatter_dime...]
    add x0 -> x4, other arithmetic: none -> 50.5 us  [local(): joined + lax.ppermute(joined, 'row', [(dev, dev ^ hop) for dev in range(1...]
  transfers between devices with their start and end apart: 8 -> 11, of which waited for: 8 -> 9; matrix products, arithmetic and copies ran while one was open for 15% -> 6% of each run, Pallas kernels for 0% -> 0%
where the time goes in v1:
time: 1590 us
  waiting for transfers between devices  1440 us (91%)
  other arithmetic  73.5 us (5%)
  matrix products  46.9 us (3%)
    ppermute x4, waiting for transfers between devices, local(): lax.ppermute(joined, 'row', [(dev, dev ^ hop) for dev in range(16)])  1280 us
    add x4, other arithmetic, local(): joined + lax.ppermute(joined, 'row', [(dev, dev ^ hop) for dev in range(1...  50.5 us
    all_gather x1, waiting for transfers between devices, local(): lax.all_gather(up_grad, 'row', axis=0, tiled=True)  45.1 us
    all_gather x1, waiting for transfers between devices, local(): lax.all_gather(gate_grad, 'row', axis=0, tiled=True)  43.4 us
  transfers between devices with their start and end apart: 11, of which 9 were waited for; matrix products, arithmetic and copies ran while one was open for 6% of the time, Pallas kernels for 0%

profile of v1, /device:TPU:0, one launch (start us, length us, event | category | flops | bytes accessed | tf_op | source)
XLA Modules:
  0.0 1591.2 jit_solution(7540246657156932345)
XLA Ops:
  8.0 27.7 %all-gather.5.cloned.1.call-done = bf16[1024,512]{1,0:T(8,128)(2,1)} async-done(((bf16[128,512]{1,0:T(8,128)(2,1)}), bf16[1024,512]{1,0:T(8,128)(2,1)}) %all-gather.5.cloned.1.call-update) | async-done | bytes 1048592 | tf_op jit(solution)/shard_map/all_gather | solution.py:20
  35.7 4.0 fusion.3
  39.7 2.1 fusion.4
  41.8 1.9 pad_maximum_fusion
  46.2 316.0 %collective-permute-done = f32[1024,3584]{1,0:T(8,128)} collective-permute-done((f32[1024,3584]{1,0:T(8,128)S(1)}, f32[1024,3584]{1,0:T(8,128)}, u32[]{:S(2)}, u32[]{:S(2)}) %collective-permute-start) | collective-permute-done | bytes 14680096 | tf_op jit(solution)/shard_map/ppermute | solution.py:32
  362.3 8.1 fusion.2
  370.3 3.1 collective-permute-start.1
  373.4 315.2 %collective-permute-done.1 = f32[1024,3584]{1,0:T(8,128)} collective-permute-done((f32[1024,3584]{1,0:T(8,128)S(1)}, f32[1024,3584]{1,0:T(8,128)}, u32[]{:S(2)}, u32[]{:S(2)}) %collective-permute-start.1) | collective-permute-done | bytes 14680096 | tf_op jit(solution)/shard_map/ppermute | solution.py:32
  688.6 10.9 add.34
  699.4 1.5 collective-permute-start.2
  701.0 314.5 %collective-permute-done.2 = f32[1024,3584]{1,0:T(8,128)} collective-permute-done((f32[1024,3584]{1,0:T(8,128)}, f32[1024,3584]{1,0:T(8,128)}, u32[]{:S(2)}, u32[]{:S(2)}) %collective-permute-start.2) | collective-permute-done | bytes 14680096 | tf_op jit(solution)/shard_map/ppermute | solution.py:32
  1015.5 15.7 add.35
  1031.2 3.0 collective-permute-start.3
  1034.2 6.3 fusion.6
  1040.6 336.8 %collective-permute-done.3 = f32[1024,3584]{1,0:T(8,128)} collective-permute-done((f32[1024,3584]{1,0:T(8,128)}, f32[1024,3584]{1,0:T(8,128)}, u32[]{:S(2)}, u32[]{:S(2)}) %collective-permute-start.3) | collective-permute-done | bytes 14680096 | tf_op jit(solution)/shard_map/ppermute | solution.py:32
  1377.4 15.9 add.36
  1393.2 15.3 slice_multiply_fusion
  1408.6 2.5 multiply_convert_fusion.1
  1411.7 5.5 fusion.5
  1417.4 43.4 %all-gather.9.cloned.1.call-done = bf16[1024,1792]{1,0:T(8,128)(2,1)} async-done(((bf16[64,1792]{1,0:T(8,128)(2,1)}), bf16[1024,1792]{1,0:T(8,128)(2,1)}) %all-gather.9.cloned.1.call-update) | async-done | bytes 3670032 | tf_op jit(solution)/shard_map/all_gather | solution.py:60
  1460.9 6.0 fusion.7
  1466.9 45.1 %all-gather.11.cloned.1.call-done = bf16[1024,1792]{1,0:T(8,128)(2,1)} async-done(((bf16[64,1792]{1,0:T(8,128)(2,1)}), bf16[1024,1792]{1,0:T(8,128)(2,1)}) %all-gather.11.cloned.1.call-update) | async-done | bytes 3670032 | tf_op jit(solution)/shard_map/all_gather | solution.py:61
  1512.0 6.6 convolution_add_fusion
  1518.6 5.7 convolution_convert_fusion
  1524.3 23.2 %reduce-scatter.4.cloned.1.call-done = f32[128,512]{1,0:T(8,128)} async-done(((f32[1024,512]{1,0:T(8,128)}), f32[128,512]{1,0:T(8,128)}) %reduce-scatter.4.cloned.1.call-update) | async-done | bytes 262160 | tf_op jit(solution)/shard_map/reduce_scatter | solution.py:44
  1547.5 1.6 convert_element_type.31
  1549.1 5.4 fusion
  1554.5 3.8 copy.10
  1558.3 5.4 fusion.1
  1563.7 3.8 copy.11
  1567.5 15.2 reduce-scatter.8.cloned.1.call-done
  1582.7 1.6 convert_element_type.34
  (25 shorter events, 4.2 us)
Async XLA Ops:
  7.2 1027.1 %copy-start = (bf16[1792,512]{1,0:T(8,128)(2,1)S(1)}, bf16[1792,512]{1,0:T(8,128)(2,1)}, u32[]{:S(2)}) copy-start(bf16[1792,512]{1,0:T(8,128)(2,1)} %param.9) | copy-start | bytes 5505028
  7.2 28.5 %all-gather.5.cloned.1.call-start = ((), (), s32[]{:S(2)}) async-start(), calls=%async_computation.3 | async-start | bytes 1179648 | tf_op jit(solution)/shard_map/all_gather | solution.py:20
  7.9 1026.3 %all-gather.7.cloned.1.call-start = ((), (), s32[]{:S(2)}) async-start(), calls=%async_computation.5 | async-start | bytes 1179648 | tf_op jit(solution)/shard_map/all_gather | solution.py:50
  35.7 4.0 copy-start.2
  35.7 4.0 copy-start.3
  41.8 2.9 copy-start.1
  44.8 317.5 %collective-permute-start = (f32[1024,3584]{1,0:T(8,128)S(1)}, f32[1024,3584]{1,0:T(8,128)}, u32[]{:S(2)}, u32[]{:S(2)}) collective-permute-start(f32[1024,3584]{1,0:T(8,128)S(1)} %pad_maximum_fusion), channel_id=1, source_target_pairs={{0,8},{8,0},{16,24},{24,16},{32,40},{40,32},{48,56},{56,48},{64,72... | collective-permute-start | bytes 44040200 | tf_op jit(solution)/shard_map/ppermute | solution.py:32
  370.3 318.2 %collective-permute-start.1 = (f32[1024,3584]{1,0:T(8,128)S(1)}, f32[1024,3584]{1,0:T(8,128)}, u32[]{:S(2)}, u32[]{:S(2)}) collective-permute-start(f32[1024,3584]{1,0:T(8,128)S(1)} %fusion.2), channel_id=1, source_target_pairs={{0,16},{8,24},{16,0},{24,8},{32,48},{40,56},{48,32},{56,40},{64,80... | collective-permute-start | bytes 44040200 | tf_op jit(solution)/shard_map/ppermute | solution.py:32
  699.4 316.0 %collective-permute-start.2 = (f32[1024,3584]{1,0:T(8,128)}, f32[1024,3584]{1,0:T(8,128)}, u32[]{:S(2)}, u32[]{:S(2)}) collective-permute-start(f32[1024,3584]{1,0:T(8,128)} %add.34), channel_id=1, source_target_pairs={{0,32},{8,40},{16,48},{24,56},{32,0},{40,8},{48,16},{56,24},{64,96... | collective-permute-start | bytes 44040200 | tf_op jit(solution)/shard_map/ppermute | solution.py:32
  701.0 707.6 %reduce-scatter.6.cloned.1.call-start = ((), (), s32[]{:S(2)}) async-start(), calls=%async_computation.6 | async-start | bytes 7798784 | tf_op jit(solution)/shard_map/reduce_scatter | solution.py:52
  1031.2 346.2 %collective-permute-start.3 = (f32[1024,3584]{1,0:T(8,128)}, f32[1024,3584]{1,0:T(8,128)}, u32[]{:S(2)}, u32[]{:S(2)}) collective-permute-start(f32[1024,3584]{1,0:T(8,128)} %add.35), channel_id=1, source_target_pairs={{0,64},{8,72},{16,80},{24,88},{32,96},{40,104},{48,112},{56,120},{... | collective-permute-start | bytes 44040200 | tf_op jit(solution)/shard_map/ppermute | solution.py:32
  1040.5 420.3 %all-gather.9.cloned.1.call-start = ((), (), s32[]{:S(2)}) async-start(), calls=%async_computation.7 | async-start | bytes 3899392 | tf_op jit(solution)/shard_map/all_gather | solution.py:60
  1411.0 101.0 %all-gather.11.cloned.1.call-start = ((), (), s32[]{:S(2)}) async-start(), calls=%async_computation.8 | async-start | bytes 3899392 | tf_op jit(solution)/shard_map/all_gather | solution.py:61
  1411.6 135.9 %reduce-scatter.4.cloned.1.call-start = ((), (), s32[]{:S(2)}) async-start(), calls=%async_computation.4 | async-start | bytes 2359296 | tf_op jit(solution)/shard_map/reduce_scatter | solution.py:44
  1417.2 165.5 %reduce-scatter.8.cloned.1.call-start = ((), (), s32[]{:S(2)}) async-start(), calls=%async_computation.9 | async-start | bytes 2359296 | tf_op jit(solution)/shard_map/reduce_scatter | solution.py:63
Sparse Core Ops, SparseCore 0:
  9.7 25.9 all-gather.4
  701.1 23.0 all-gather.6
  1040.6 360.5 reduce-scatter.5
  1411.2 49.6 all-gather.8
  1463.4 48.5 all-gather.10
  1514.3 33.1 reduce-scatter.3
  1549.9 32.7 reduce-scatter.7
